TPU v7x, 32 devices: a whole 2x2x4 slice. The times are simulated.
32 devices in a mesh: clip: 2 (over y), tm: 8 (over z, x), tile: 2 (over core).
Axes of the slice: x: 2, y: 2, z: 4, core: 2. Of those that a mesh axis runs over, the one named last changes fastest.
Arguments:
- queries: bfloat16 [32, 256, 2048], P(('clip', 'tm'), 'tile'), parts along dimension 0, may hold values from -48 to 48
- keyvals: bfloat16 [2, 32, 256, 512], P(None, ('clip', 'tm'), 'tile'), parts along dimension 1, may hold values from -4 to 4
- proj_weight: bfloat16 [2048, 1024], P('tm', 'tile'), may hold values from -0.125 to 0.125
- norm_gain: float32 [1024], P('tile'), may hold values from 0.25 to 1.75
- frame_counts: int32 [32], P(('clip', 'tm')), parts along dimension 0, may hold values from 129 to 256, as said below
Outputs:
- dynamics: bfloat16 [32, 256, 1024], P(('clip', 'tm'), None, 'tile'), parts along dimension 0
There are 2 independent parts, one for each index of `clip`. A program takes and returns all parts, laid end to end along the dimension named above; an argument that names none is the same for every part. Nothing has to cross between parts.
Inputs may be any that keep to these rules, and one draw needn't show every extreme that they name: `frame_counts`: every spatial tile of every frame holds a live slot; some frame is full.
All inputs are finite; a program needn't handle non-finite values.
Results may differ from a plain program's by a relative error of at most 0.013.
Values may be sent and summed in bfloat16 or wider, within the bound.
No kernel may reach another device: no remote copies, remote signals or barrier semaphores. Data moves between devices by JAX's collectives and lax.ppermute only.
A program may use at most 64 MiB of HBM per device.

v0:
```python
import jax
import jax.numpy as jnp
from jax import lax
from jax.sharding import PartitionSpec as P

QHEADS = 16
KVHEADS = 4
HEAD_DIM = 128
IDM_DIM = 64
WINDOW = 4
PARTNER = 16


def passed_along(value, axis, steps):
    count = lax.axis_size(axis)
    initial, last = (max(0, -steps), min(count, count - steps))
    return lax.ppermute(value, axis, [(source, source + steps) for source in range(initial, last)])


def window_attention(query_block, key_block, value_block, live_keys, groups):
    row_count = query_block.shape[0]
    key_heads = key_block.shape[1]
    head_width = key_block.shape[2]
    grouped = query_block.reshape(row_count, key_heads, groups, head_width)
    scores = jnp.einsum(
        "ikgd,jkd->ikgj", grouped, key_block, preferred_element_type=jnp.float32
    ) * head_width ** (-0.5)
    key_mask = live_keys[None, None, None, :]
    row_max = jnp.max(jnp.where(key_mask, scores, -1e30), axis=-1, keepdims=True)
    weights = jnp.where(key_mask, jnp.exp(jnp.where(key_mask, scores, row_max) - row_max), 0.0)
    normalized = (weights / jnp.sum(weights, axis=-1, keepdims=True)).astype(jnp.bfloat16)
    blended = jnp.einsum(
        "ikgj,jkd->ikgd", normalized, value_block, preferred_element_type=jnp.float32
    )
    return blended.astype(jnp.bfloat16).reshape(row_count, key_heads * groups * head_width)


def normalize_heads(latent_block, gain):
    width = latent_block.shape[-1]
    heads = width // IDM_DIM
    values = latent_block.astype(jnp.float32).reshape(latent_block.shape[:-1] + (heads, IDM_DIM))
    scaled = values * lax.rsqrt(jnp.mean(values * values, axis=-1, keepdims=True) + 1e-06)
    scaled = scaled * gain.reshape(heads, IDM_DIM)
    return scaled.astype(jnp.bfloat16).reshape(latent_block.shape)


def local(queries, keyvals, proj_weight, norm_gain, frame_counts):
    frames_here = queries.shape[0]
    tile_tokens = queries.shape[1]
    groups = QHEADS // KVHEADS
    lead_frames = WINDOW - 1
    hop_total = (lead_frames + frames_here - 1) // frames_here
    tile_place = lax.axis_index("tile")
    received = []
    for hop_count in range(1, hop_total + 1):
        needed = min(frames_here, lead_frames - (hop_count - 1) * frames_here)
        piece_pair = passed_along(
            (keyvals[:, frames_here - needed :], frame_counts[frames_here - needed :]),
            "tm",
            hop_count,
        )
        received = [piece_pair] + received
    earlier_kv = jnp.concatenate([received_pair[0] for received_pair in received], axis=1)
    earlier_counts = jnp.concatenate([received_pair[1] for received_pair in received], axis=0)
    window_kv = jnp.concatenate([earlier_kv, keyvals], axis=1)
    window_counts = jnp.concatenate([earlier_counts, frame_counts], axis=0)
    slot_index = tile_place * tile_tokens + jnp.arange(tile_tokens, dtype=jnp.int32)
    attended_frames = []
    for frame_index in range(frames_here):
        block_kv = window_kv[:, frame_index : frame_index + WINDOW]
        live_keys = (
            slot_index[None, :] < window_counts[frame_index : frame_index + WINDOW, None]
        ).reshape(WINDOW * tile_tokens)
        key_block = block_kv[0].reshape(WINDOW * tile_tokens, KVHEADS, HEAD_DIM)
        value_block = block_kv[1].reshape(WINDOW * tile_tokens, KVHEADS, HEAD_DIM)
        attended_frames.append(
            window_attention(queries[frame_index], key_block, value_block, live_keys, groups)
        )
    attended = jnp.stack(attended_frames)
    query_width = attended.shape[2]
    full_columns = lax.all_gather(proj_weight, "tile", axis=1, tiled=True)
    token_rows = attended.reshape(frames_here * tile_tokens, query_width)
    summed = jnp.dot(
        token_rows,
        lax.all_gather(full_columns, "tm", axis=0, tiled=True),
        preferred_element_type=jnp.float32,
    )
    own_latent = summed.astype(jnp.bfloat16).reshape(
        frames_here, tile_tokens, full_columns.shape[1]
    )
    latent = lax.all_to_all(own_latent, "tile", split_axis=2, concat_axis=1, tiled=True)
    normed = normalize_heads(latent, norm_gain)
    frame_tokens = normed.shape[1]
    heads_here = normed.shape[2] // IDM_DIM
    distance = PARTNER // frames_here
    before_normed, before_counts = passed_along((normed, frame_counts), "tm", distance)
    after_normed, after_counts = passed_along((normed, frame_counts), "tm", -distance)
    slot_all = jnp.arange(frame_tokens, dtype=jnp.int32)
    results = []
    for frame_index in range(frames_here):
        key_rows = jnp.concatenate(
            [before_normed[frame_index], normed[frame_index], after_normed[frame_index]], axis=0
        )
        key_rows = key_rows.reshape(3 * frame_tokens, heads_here, IDM_DIM)
        live_keys = jnp.concatenate(
            [
                slot_all < before_counts[frame_index],
                slot_all < frame_counts[frame_index],
                slot_all < after_counts[frame_index],
            ]
        )
        query_rows = normed[frame_index].reshape(frame_tokens, heads_here, IDM_DIM)
        scores = jnp.einsum(
            "ihd,jhd->ihj", query_rows, key_rows, preferred_element_type=jnp.float32
        ) * IDM_DIM ** (-0.5)
        weights = jnp.where(live_keys[None, None, :], jnp.exp(scores), 0.0)
        normalized = (weights / jnp.sum(weights, axis=-1, keepdims=True)).astype(jnp.bfloat16)
        blended = jnp.einsum(
            "ihj,jhd->ihd", normalized, key_rows, preferred_element_type=jnp.float32
        )
        results.append(blended.astype(jnp.bfloat16).reshape(frame_tokens, heads_here * IDM_DIM))
    return jnp.stack(results)


def solution(mesh):
    in_specs = (
        P(("clip", "tm"), "tile", None),
        P(None, ("clip", "tm"), "tile", None),
        P("tm", "tile"),
        P("tile"),
        P(("clip", "tm")),
    )
    out_specs = P(("clip", "tm"), None, "tile")
    return jax.shard_map(local, mesh=mesh, in_specs=in_specs, out_specs=out_specs, check_vma=False)
```

profile of v0, /device:TPU:0, one launch (start us, length us, event | category | flops | bytes accessed | tf_op | source)
XLA Modules:
  0.0 124.8 jit_solution(14114580612585396030)
XLA Ops:
  6.5 4.3 %all_gather.6 = bf16[256,1024]{1,0:T(8,128)(2,1)} all-gather(bf16[256,512]{1,0:T(8,128)(2,1)} %param.7), channel_id=1, replica_groups=mesh['clip'=2,'tm'=8,'tile'=2] {'tile'}, dimensions={1}, use_global_device_ids=true | all-gather | bytes 786432 | tf_op jit(solution)/shard_map/all_gather | solution.py:81
  10.9 4.5 %collective-permute-start.3 = (s32[2]{0:T(128)}, s32[2]{0:T(128)S(1)}, u32[]{:S(2)}, u32[]{:S(2)}) collective-permute-start(s32[2]{0:T(128)} %param.9), channel_id=1, source_target_pairs={{0,2},{2,4},{4,6},{6,8},{8,10},{10,12},{12,14},{1,3},{3,5},{5,7},{... | collective-permute-start | bytes 32 | tf_op jit(solution)/shard_map/ppermute | solution.py:17
  15.4 0.7 collective-permute-start.5
  16.1 3.5 %collective-permute-start.1 = (bf16[2,2,128,512]{3,2,1,0:T(8,128)(2,1)}, bf16[2,2,128,512]{3,2,1,0:T(8,128)(2,1)S(1)}, u32[]{:S(2)}, u32[]{:S(2)}) collective-permute-start(bf16[2,2,128,512]{3,2,1,0:T(8,128)(2,1)} %param.6), channel_id=1, source_target_pairs={{0,2},{2,4},{4,6},{6,8},{8,10},{10,12},{12,14},{1,3},{3,5},{5,7},{... | collective-permute-start | bytes 1572872 | tf_op jit(solution)/shard_map/ppermute | solution.py:17
  19.6 1.0 slice.65
  20.6 3.5 %collective-permute-start = (bf16[2,1,128,512]{3,2,1,0:T(8,128)(2,1)S(1)}, bf16[2,1,128,512]{3,2,1,0:T(8,128)(2,1)S(1)}, u32[]{:S(2)}, u32[]{:S(2)}) collective-permute-start(bf16[2,1,128,512]{3,2,1,0:T(8,128)(2,1)S(1)} %slice.65), channel_id=1, source_target_pairs={{0,4},{2,6},{4,8},{6,10},{8,12},{10,14},{1,5},{3,7},{5,9},{7,11},{... | collective-permute-start | bytes 786440 | tf_op jit(solution)/shard_map/ppermute | solution.py:17
  24.0 1.4 %fusion.52 = (s32[1]{0:T(128)}, s32[1]{0:T(128)}) fusion(s32[2]{0:T(128)} %param.9), kind=kLoop, calls=%fused_computation.86 | loop fusion | bytes 16 | tf_op jit(solution)/shard_map/slice | solution.py:108
  25.4 4.0 %collective-permute-start.2 = (s32[1]{0:T(128)}, s32[1]{0:T(128)}, u32[]{:S(2)}, u32[]{:S(2)}) collective-permute-start(s32[1]{0:T(128)} %get-tuple-element.20), channel_id=1, source_target_pairs={{0,4},{2,6},{4,8},{6,10},{8,12},{10,14},{1,5},{3,7},{5,9},{7,11},{... | collective-permute-start | bytes 20 | tf_op jit(solution)/shard_map/ppermute | solution.py:17
  29.4 1.3 %fusion.49 = (bf16[1,128,2048]{2,1,0:T(8,128)(2,1)S(1)}, bf16[1,128,2048]{2,1,0:T(8,128)(2,1)S(1)}) fusion(bf16[2,128,2048]{2,1,0:T(8,128)(2,1)} %param.5), kind=kLoop, calls=%fused_computation.83 | loop fusion | bytes 2097152 | tf_op jit(solution)/shard_map/slice | solution.py:77
  32.0 0.7 fusion.53
  32.7 0.7 iota_compare_fusion.1
  33.4 1.3 %iota_compare_fusion.2 = (pred[256]{0:T(512)(128)(4,1)S(1)}, pred[256]{0:T(512)(128)(4,1)S(1)}) fusion(s32[]{:T(128)} %bitcast.22, s32[]{:T(128)} %bitcast.21), kind=kLoop, calls=%fused_computation.65 | loop fusion | flops 512 | bytes 520 | tf_op jit(solution)/shard_map/lt | solution.py:108
  34.8 1.2 collective-permute-done.2
  36.0 0.8 pad_add_fusion.2
  37.3 0.9 reshape_squeeze.21
  38.3 1.8 %fusion.6 = (f32[128,4,4]{0,2,1:T(4,128)S(1)}, f32[4,512,128,4]{2,1,3,0:T(8,128)S(1)}) fusion(pred[512]{0:T(512)(128)(4,1)S(1)} %get-tuple-element.23, bf16[128,4,4,128]{0,3,2,1:T(8,128)(2,1)S(1)} %bitcast.120, bf16[512,4,128,1]{2,1,0,3:T(4,128)(2,1)} %bitcast.122), kind=kOutput, calls=%fused_computation.16 | convolution fusion | flops 271579136 | bytes 5251584 | tf_op jit(solution)/shard_map/ikgd,jkd->ikgj/dot_general | solution.py:25
  40.1 1.1 fusion.14
  41.2 1.4 %fusion.19 = bf16[4,128,128,4]{2,1,3,0:T(8,128)(2,1)S(1)} fusion(f32[4,512,128,4]{2,1,3,0:T(8,128)S(1)} %get-tuple-element.28, f32[128,4,4]{0,2,1:T(4,128)S(1)} %fusion.14, f32[128,4,4]{0,2,1:T(4,128)S(1)} %get-tuple-element.27, pred[512]{0:T(512)(128)(4,1)S(1)} %get-tuple-element.23, bf16[512,4,128,1]{2,1,0,3:T(4,128)(2,1)S(1)} %bitcast.125), kind=kOutput, calls=%fused_computation.29 | convolution fusion | flops 274989056 | bytes 5259776 | tf_op jit(solution)/shard_map/ikgj,jkd->ikgd/dot_general | solution.py:32
  43.1 0.8 fusion.2
  43.9 1.1 fusion.15
  45.0 1.4 %fusion.18 = bf16[4,128,128,4]{2,1,3,0:T(8,128)(2,1)S(1)} fusion(f32[4,512,128,4]{2,1,3,0:T(8,128)S(1)} %get-tuple-element.26, f32[128,4,4]{0,2,1:T(4,128)S(1)} %fusion.15, f32[128,4,4]{0,2,1:T(4,128)S(1)} %get-tuple-element.25, pred[512]{0:T(512)(128)(4,1)S(1)} %get-tuple-element.24, bf16[512,4,128,1]{2,1,0,3:T(4,128)(2,1)S(1)} %bitcast.124), kind=kOutput, calls=%fused_computation.28 | convolution fusion | flops 274989056 | bytes 5259776 | tf_op jit(solution)/shard_map/ikgj,jkd->ikgd/dot_general | solution.py:32
  46.7 52.3 %all-gather.2.cloned.1.call-done = bf16[2048,1024]{1,0:T(8,128)(2,1)} async-done(((bf16[256,1024]{1,0:T(8,128)(2,1)}), bf16[2048,1024]{1,0:T(8,128)(2,1)}) %all-gather.2.cloned.1.call-update) | async-done | bytes 4194320 | tf_op jit(solution)/shard_map/all_gather | solution.py:85
  99.0 3.5 %convolution_convert_fusion = bf16[256,1024]{1,0:T(8,128)(2,1)S(1)} fusion(bf16[256,2048]{1,0:T(8,128)(2,1)S(1)} %bitcast.123, bf16[2048,1024]{1,0:T(8,128)(2,1)} %all-gather.2.cloned.1.call-done), kind=kOutput, calls=%fused_computation.30 | convolution fusion | flops 1074003968 | bytes 5767168 | tf_op jit(solution)/shard_map/dot_general | solution.py:83
  102.9 4.2 %all_to_all.4 = bf16[2,128,1024]{1,0,2:T(2,128)(2,1)S(1)} all-to-all(bf16[2,128,1024]{1,0,2:T(2,128)(2,1)S(1)} %copy.44), channel_id=1, replica_groups=mesh['clip'=2,'tm'=8,'tile'=2] {'tile'}, dimensions={2} | all-to-all | bytes 1048576 | tf_op jit(solution)/shard_map/all_to_all | solution.py:91
  107.6 0.8 reshape.95
  108.5 0.8 reshape.94
  109.6 0.7 collective-permute-start.4
  110.6 1.6 %bitcast_reduce_fusion.1 = (f32[256,8]{0,1:T(8,128)S(1)}, f32[8,768,256]{2,1,0:T(8,128)S(1)}) fusion(pred[768]{0:T(1024)(128)(4,1)S(1)} %pad_add_fusion, bf16[256,8,64]{0,2,1:T(8,128)(2,1)S(1)} %get-tuple-element.13, bf16[256,8,64]{0,2,1:T(8,128)(2,1)S(1)} %bitcast.133), kind=kOutput, calls=%fused_computation.4 | convolution fusion | flops 208402432 | bytes 6824704 | tf_op jit(solution)/shard_map/ihd,jhd->ihj/dot_general | solution.py:113
  112.3 1.5 %fusion.23 = bf16[8,64,256]{2,1,0:T(8,128)(2,1)S(1)} fusion(f32[8,768,256]{2,1,0:T(8,128)S(1)} %get-tuple-element.32, f32[256,8]{0,1:T(8,128)S(1)} %get-tuple-element.31, pred[768]{0:T(1024)(128)(4,1)S(1)} %pad_add_fusion, bf16[256,8,64]{0,2,1:T(8,128)(2,1)S(1)} %bitcast.134, bf16[256,8,64]{0,2,1:T(8,128)(2,1)S(1)} %get-tuple-element.13), kind=kOutput, calls=%fused_computation.32 | convolution fusion | flops 210108416 | bytes 7086848 | tf_op jit(solution)/shard_map/ihj,jhd->ihd/dot_general | solution.py:118
  113.9 1.6 %bitcast_reduce_fusion = (f32[256,8]{0,1:T(8,128)S(1)}, f32[8,768,256]{2,1,0:T(8,128)S(1)}) fusion(pred[768]{0:T(1024)(128)(4,1)S(1)} %pad_add_fusion.1, bf16[256,8,64]{0,2,1:T(8,128)(2,1)S(1)} %get-tuple-element.14, bf16[256,8,64]{0,2,1:T(8,128)(2,1)S(1)} %bitcast.131), kind=kOutput, calls=%fused_computation.1 | convolution fusion | flops 208402432 | bytes 6824704 | tf_op jit(solution)/shard_map/ihd,jhd->ihj/dot_general | solution.py:113
  115.5 1.5 %fusion.20 = bf16[8,64,256]{2,1,0:T(8,128)(2,1)S(1)} fusion(f32[8,768,256]{2,1,0:T(8,128)S(1)} %get-tuple-element.30, f32[256,8]{0,1:T(8,128)S(1)} %get-tuple-element.29, pred[768]{0:T(1024)(128)(4,1)S(1)} %pad_add_fusion.1, bf16[256,8,64]{0,2,1:T(8,128)(2,1)S(1)} %bitcast.132, bf16[256,8,64]{0,2,1:T(8,128)(2,1)S(1)} %get-tuple-element.14), kind=kOutput, calls=%fused_computation.31 | convolution fusion | flops 210108416 | bytes 7086848 | tf_op jit(solution)/shard_map/ihj,jhd->ihd/dot_general | solution.py:118
  117.1 0.8 pad_maximum_fusion.7
  (42 shorter events, 4.6 us)
Async XLA Ops:
  6.5 28.2 %copy-start.2 = (s32[2]{0:T(128)S(1)}, s32[2]{0:T(128)}, u32[]{:S(2)}) copy-start(s32[2]{0:T(128)} %param.9) | copy-start | bytes 28
  6.5 30.4 %copy-start = (bf16[2,2,128,512]{3,2,1,0:T(8,128)(2,1)S(1)}, bf16[2,2,128,512]{3,2,1,0:T(8,128)(2,1)}, u32[]{:S(2)}) copy-start(bf16[2,2,128,512]{3,2,1,0:T(8,128)(2,1)} %param.6) | copy-start | bytes 1572868
  6.5 24.8 %copy-start.1 = (f32[512]{0:T(512)S(1)}, f32[512]{0:T(512)}, u32[]{:S(2)}) copy-start(f32[512]{0:T(512)} %param.8) | copy-start | bytes 6148
  6.5 92.5 %all-gather.2.cloned.1.call-start = ((), (), s32[]{:S(2)}) async-start(), calls=%async_computation.1 | async-start | bytes 4718592 | tf_op jit(solution)/shard_map/all_gather | solution.py:85
  10.9 23.8 %collective-permute-start.3 = (s32[2]{0:T(128)}, s32[2]{0:T(128)S(1)}, u32[]{:S(2)}, u32[]{:S(2)}) collective-permute-start(s32[2]{0:T(128)} %param.9), channel_id=1, source_target_pairs={{0,2},{2,4},{4,6},{6,8},{8,10},{10,12},{12,14},{1,3},{3,5},{5,7},{... | collective-permute-start | bytes 32 | tf_op jit(solution)/shard_map/ppermute | solution.py:17
  15.4 16.6 %collective-permute-start.5 = (s32[2]{0:T(128)}, s32[2]{0:T(128)S(1)}, u32[]{:S(2)}, u32[]{:S(2)}) collective-permute-start(s32[2]{0:T(128)} %param.9), channel_id=1, source_target_pairs={} | collective-permute-start | bytes 32 | tf_op jit(solution)/shard_map/ppermute | solution.py:17
  16.1 20.8 %collective-permute-start.1 = (bf16[2,2,128,512]{3,2,1,0:T(8,128)(2,1)}, bf16[2,2,128,512]{3,2,1,0:T(8,128)(2,1)S(1)}, u32[]{:S(2)}, u32[]{:S(2)}) collective-permute-start(bf16[2,2,128,512]{3,2,1,0:T(8,128)(2,1)} %param.6), channel_id=1, source_target_pairs={{0,2},{2,4},{4,6},{6,8},{8,10},{10,12},{12,14},{1,3},{3,5},{5,7},{... | collective-permute-start | bytes 1572872 | tf_op jit(solution)/shard_map/ppermute | solution.py:17
  20.6 16.3 %collective-permute-start = (bf16[2,1,128,512]{3,2,1,0:T(8,128)(2,1)S(1)}, bf16[2,1,128,512]{3,2,1,0:T(8,128)(2,1)S(1)}, u32[]{:S(2)}, u32[]{:S(2)}) collective-permute-start(bf16[2,1,128,512]{3,2,1,0:T(8,128)(2,1)S(1)} %slice.65), channel_id=1, source_target_pairs={{0,4},{2,6},{4,8},{6,10},{8,12},{10,14},{1,5},{3,7},{5,9},{7,11},{... | collective-permute-start | bytes 786440 | tf_op jit(solution)/shard_map/ppermute | solution.py:17
  25.4 10.6 %collective-permute-start.2 = (s32[1]{0:T(128)}, s32[1]{0:T(128)}, u32[]{:S(2)}, u32[]{:S(2)}) collective-permute-start(s32[1]{0:T(128)} %get-tuple-element.20), channel_id=1, source_target_pairs={{0,4},{2,6},{4,8},{6,10},{8,12},{10,14},{1,5},{3,7},{5,9},{7,11},{... | collective-permute-start | bytes 20 | tf_op jit(solution)/shard_map/ppermute | solution.py:17
  109.6 0.9 collective-permute-start.4
Sparse Core Ops, SparseCore 0:
  11.0 87.9 all-gather.1
where the time goes:
time: 125 us
  waiting for transfers between devices  53.5 us (43%)
  starting transfers between devices  16.8 us (13%)
  matrix products  15.1 us (12%)
  between operations  13.8 us (11%)
  local copies, waits for them, and re-layouts  10 us (8%)
  blocking collectives  8.49 us (7%)
  other arithmetic  7.11 us (6%)
    all_gather x1, waiting for transfers between devices, local(): lax.all_gather(full_columns, 'tm', axis=0, tiled=True)  52.3 us
    ppermute x6, starting transfers between devices, passed_along(): lax.ppermute(value, axis, [(source, source + steps) for source in range(i...  16.8 us
    all_gather x1, blocking collectives, local(): full_columns = lax.all_gather(proj_weight, 'tile', axis=1, tiled=True)  4.34 us
    all_to_all x1, blocking collectives, local(): lax.all_to_all(own_latent, 'tile', split_axis=2, concat_axis=1, tiled=True)  4.15 us
    dot_general x1, matrix products, local(): jnp.dot(token_rows, lax.all_gather(full_columns, 'tm', axis=0, tiled=True...  3.49 us
    dot_general x2, matrix products, local(): jnp.einsum('ihd,jhd->ihj', query_rows, key_rows, preferred_element_type=j...  3.23 us
    dot_general x2, matrix products, local(): jnp.einsum('ihj,jhd->ihd', normalized, key_rows, preferred_element_type=j...  2.96 us
    dot_general x2, matrix products, window_attention(): jnp.einsum('ikgj,jkd->ikgd', normalized, value_block, preferred_element_t...  2.82 us
  transfers between devices with their start and end apart: 7, of which 2 were waited for; matrix products, arithmetic and copies ran while one was open for 15% of the time, Pallas kernels for 0%

commit v1 on v0

--- a/solution.py
+++ b/solution.py
@@ -9,6 +9,17 @@
 IDM_DIM = 64
 WINDOW = 4
 PARTNER = 16
+
+
+def obtain_scales(z_in, array_dim):
+    z_in = jnp.moveaxis(z_in, 0, array_dim)
+    work_now = z_in.shape
+    near = z_in.reshape(
+        *work_now[:array_dim],
+        work_now[array_dim] * work_now[array_dim + 1],
+        *work_now[array_dim + 2 :]
+    )
+    return near
 
 
 def passed_along(value, axis, steps):
@@ -45,6 +56,31 @@
 
 
 def local(queries, keyvals, proj_weight, norm_gain, frame_counts):
+
+    def _touch_state(page, mesh_dim, k_dim):
+        sides = lax.axis_size(mesh_dim)
+        rows = [(c, (c + 1) % sides) for c in range(sides)]
+        all_rows, later = ([], [])
+        in_order = [(w, at) for at, w in rows]
+        for q in range(sides - 1):
+            if q % 2 == 0:
+                mid_arr = lax.ppermute(
+                    all_rows[-1] if all_rows else page, axis_name=mesh_dim, perm=rows
+                )
+                all_rows.append(mid_arr)
+            else:
+                oldest = lax.ppermute(
+                    later[-1] if later else page, axis_name=mesh_dim, perm=in_order
+                )
+                later.append(oldest)
+        view_out = jnp.stack([*all_rows[::-1], page, *later], 0)
+        built = len(all_rows)
+        f_now = lax.axis_index(mesh_dim)
+        low = f_now - built
+        view_out = view_out[(jnp.arange(sides) - low) % sides]
+        block_now = obtain_scales(view_out, k_dim)
+        return block_now
+
     frames_here = queries.shape[0]
     tile_tokens = queries.shape[1]
     groups = QHEADS // KVHEADS
@@ -81,9 +117,7 @@
     full_columns = lax.all_gather(proj_weight, "tile", axis=1, tiled=True)
     token_rows = attended.reshape(frames_here * tile_tokens, query_width)
     summed = jnp.dot(
-        token_rows,
-        lax.all_gather(full_columns, "tm", axis=0, tiled=True),
-        preferred_element_type=jnp.float32,
+        token_rows, _touch_state(full_columns, "tm", k_dim=0), preferred_element_type=jnp.float32
     )
     own_latent = summed.astype(jnp.bfloat16).reshape(
         frames_here, tile_tokens, full_columns.shape[1]

time: 125 us -> 149 us (1.19)
  starting transfers between devices: 16.8 us -> 40.5 us
  local copies, waits for them, and re-layouts: 10 us -> 28.6 us
  between operations: 13.8 us -> 0.44 us
  waiting for transfers between devices: 53.5 us -> 40.9 us
  matrix products: 15.1 us -> 19.7 us
  other arithmetic: 7.11 us -> 11.4 us
  blocking collectives: 8.49 us -> 6.53 us
    all_gather x1 -> x0, waiting for transfers between devices: 52.3 us -> none  [local(): lax.all_gather(full_columns, 'tm', axis=0, tiled=True)]
    ppermute x0 -> x7, waiting for transfers between devices: none -> 28.8 us  [the longest x4 28.4 us: _touch_state(): lax.ppermute(all_rows[-1] if all_rows else page, axis_name=mesh_dim, perm...]
    ppermute x0 -> x7, starting transfers between devices: none -> 25.4 us  [the longest x3 21.2 us: _touch_state(): lax.ppermute(later[-1] if later else page, axis_name=mesh_dim, perm=in_or...]
    unnamed x10 -> x23, local copies, waits for them, and re-layouts: 0.68 us -> 11.8 us
    ppermute x6, waiting for transfers between devices: 1.24 us -> 12.1 us  [passed_along(): lax.ppermute(value, axis, [(source, source + steps) for source in range(i...]
    gather x0 -> x1, local copies, waits for them, and re-layouts: none -> 4.96 us  [_touch_state(): view_out = view_out[(jnp.arange(sides) - low) % sides]]
    reduce_sum x2, other arithmetic: 2.14 us -> 6.65 us  [window_attention(): jnp.sum(weights, axis=-1, keepdims=True)]
    dot_general x2, matrix products: 2.59 us -> 6.46 us  [window_attention(): jnp.einsum('ikgd,jkd->ikgj', grouped, key_block, preferred_element_type=j...]
  transfers between devices with their start and end apart: 7 -> 13, of which waited for: 2 -> 5; matrix products, arithmetic and copies ran while one was open for 15% -> 27% of each run, Pallas kernels for 0% -> 0%
where the time goes in v1:
time: 149 us; the launch traced here: 148 us
  waiting for transfers between devices  40.9 us (27%)
  starting transfers between devices  40.5 us (27%)
  local copies, waits for them, and re-layouts  28.6 us (19%)
  matrix products  19.7 us (13%)
  other arithmetic  11.4 us (8%)
  blocking collectives  6.53 us (4%)
    ppermute x4, waiting for transfers between devices, _touch_state(): lax.ppermute(all_rows[-1] if all_rows else page, axis_name=mesh_dim, perm...  28.4 us
    ppermute x3, starting transfers between devices, _touch_state(): lax.ppermute(later[-1] if later else page, axis_name=mesh_dim, perm=in_or...  21.2 us
    ppermute x6, starting transfers between devices, passed_along(): lax.ppermute(value, axis, [(source, source + steps) for source in range(i...  15.1 us
    ppermute x6, waiting for transfers between devices, passed_along(): lax.ppermute(value, axis, [(source, source + steps) for source in range(i...  12.1 us
    unnamed x23, local copies, waits for them, and re-layouts  11.8 us
    reduce_sum x2, other arithmetic, window_attention(): jnp.sum(weights, axis=-1, keepdims=True)  6.65 us
    dot_general x2, matrix products, window_attention(): jnp.einsum('ikgd,jkd->ikgj', grouped, key_block, preferred_element_type=j...  6.46 us
    gather x1, local copies, waits for them, and re-layouts, _touch_state(): view_out = view_out[(jnp.arange(sides) - low) % sides]  4.96 us
  transfers between devices with their start and end apart: 13, of which 5 were waited for; matrix products, arithmetic and copies ran while one was open for 27% of the time, Pallas kernels for 0%

profile of v1, /device:TPU:0, one launch (start us, length us, event | category | flops | bytes accessed | tf_op | source)
XLA Modules:
  0.0 148.2 jit_solution(4093792330601904988)
XLA Ops:
  0.0 5.0 %collective-permute-start.3 = (s32[2]{0:T(128)}, s32[2]{0:T(128)S(1)}, u32[]{:S(2)}, u32[]{:S(2)}) collective-permute-start(s32[2]{0:T(128)} %param.9), channel_id=1, source_target_pairs={{0,2},{2,4},{4,6},{6,8},{8,10},{10,12},{12,14},{1,3},{3,5},{5,7},{... | collective-permute-start | bytes 32 | tf_op jit(solution)/shard_map/ppermute | solution.py:28
  5.7 3.5 %collective-permute-start.1 = (bf16[2,2,128,512]{3,2,1,0:T(8,128)(2,1)}, bf16[2,2,128,512]{3,2,1,0:T(8,128)(2,1)S(1)}, u32[]{:S(2)}, u32[]{:S(2)}) collective-permute-start(bf16[2,2,128,512]{3,2,1,0:T(8,128)(2,1)} %param.6), channel_id=1, source_target_pairs={{0,2},{2,4},{4,6},{6,8},{8,10},{10,12},{12,14},{1,3},{3,5},{5,7},{... | collective-permute-start | bytes 1572872 | tf_op jit(solution)/shard_map/ppermute | solution.py:28
  10.5 4.0 %collective-permute-start.2 = (s32[1]{0:T(128)}, s32[1]{0:T(128)}, u32[]{:S(2)}, u32[]{:S(2)}) collective-permute-start(s32[1]{0:T(128)} %get-tuple-element.20), channel_id=1, source_target_pairs={{0,4},{2,6},{4,8},{6,10},{8,12},{10,14},{1,5},{3,7},{5,9},{7,11},{... | collective-permute-start | bytes 20 | tf_op jit(solution)/shard_map/ppermute | solution.py:28
  14.5 2.4 %all_gather.3 = bf16[256,1024]{1,0:T(8,128)(2,1)S(1)} all-gather(bf16[256,512]{1,0:T(8,128)(2,1)} %param.7), channel_id=1, replica_groups=mesh['clip'=2,'tm'=8,'tile'=2] {'tile'}, dimensions={1}, use_global_device_ids=true | all-gather | bytes 786432 | tf_op jit(solution)/shard_map/all_gather | solution.py:117
  16.9 1.5 %collective-permute-start.4 = (bf16[256,1024]{1,0:T(8,128)(2,1)S(1)}, bf16[256,1024]{1,0:T(8,128)(2,1)}, u32[]{:S(2)}, u32[]{:S(2)}) collective-permute-start(bf16[256,1024]{1,0:T(8,128)(2,1)S(1)} %all_gather.3), channel_id=1, source_target_pairs={{0,2},{2,4},{4,6},{6,8},{8,10},{10,12},{12,14},{14,0},{1,3},{3,5},... | collective-permute-start | bytes 1572872 | tf_op jit(solution)/shard_map/ppermute | solution.py:67
  21.9 3.3 %collective-permute-start.8 = (bf16[256,1024]{1,0:T(8,128)(2,1)S(1)}, bf16[256,1024]{1,0:T(8,128)(2,1)}, u32[]{:S(2)}, u32[]{:S(2)}) collective-permute-start(bf16[256,1024]{1,0:T(8,128)(2,1)S(1)} %all_gather.3), channel_id=1, source_target_pairs={{2,0},{4,2},{6,4},{8,6},{10,8},{12,10},{14,12},{0,14},{3,1},{5,3},... | collective-permute-start | bytes 1572872 | tf_op jit(solution)/shard_map/ppermute | solution.py:72
  29.9 12.1 %collective-permute-done = bf16[2,1,128,512]{3,2,1,0:T(8,128)(2,1)S(1)} collective-permute-done((bf16[2,1,128,512]{3,2,1,0:T(8,128)(2,1)S(1)}, bf16[2,1,128,512]{3,2,1,0:T(8,128)(2,1)S(1)}, u32[]{:S(2)}, u32[]{:S(2)}) %collective-permute-start) | collective-permute-done | bytes 262176 | tf_op jit(solution)/shard_map/ppermute | solution.py:28
  43.2 2.0 %reshape_squeeze.21 = bf16[512,4,128]{2,1,0:T(4,128)(2,1)} reshape(bf16[1,4,128,512]{3,2,1,0:T(8,128)(2,1)} %get-tuple-element.6) | data formatting | bytes 1048576 | tf_op jit(solution)/shard_map/reshape;squeeze | solution.py:110
  45.2 3.7 %fusion.6 = (f32[128,4,4]{0,2,1:T(4,128)S(1)}, f32[4,512,128,4]{2,1,3,0:T(8,128)}) fusion(pred[512]{0:T(512)(128)(4,1)S(1)} %get-tuple-element.23, bf16[128,4,4,128]{0,3,2,1:T(8,128)(2,1)S(1)} %bitcast.140, bf16[512,4,128,1]{2,1,0,3:T(4,128)(2,1)} %bitcast.142), kind=kOutput, calls=%fused_computation.17 | convolution fusion | flops 271579136 | bytes 5251584 | tf_op jit(solution)/shard_map/ikgd,jkd->ikgj/dot_general | solution.py:36
  49.1 3.4 %fusion.14 = f32[128,4,4]{0,2,1:T(4,128)S(1)} fusion(f32[4,512,128,4]{2,1,3,0:T(8,128)} %get-tuple-element.28, f32[128,4,4]{0,2,1:T(4,128)S(1)} %get-tuple-element.27, pred[512]{0:T(512)(128)(4,1)S(1)} %get-tuple-element.23), kind=kLoop, calls=%fused_computation.25 | loop fusion | flops 5240832 | bytes 4211200 | tf_op jit(solution)/shard_map/reduce_sum | solution.py:42
  52.6 2.2 %fusion.19 = bf16[4,128,128,4]{2,1,3,0:T(8,128)(2,1)} fusion(f32[4,512,128,4]{2,1,3,0:T(8,128)S(1)} %copy-done.1, f32[128,4,4]{0,2,1:T(4,128)S(1)} %fusion.14, f32[128,4,4]{0,2,1:T(4,128)S(1)} %get-tuple-element.27, pred[512]{0:T(512)(128)(4,1)S(1)} %get-tuple-element.23, bf16[512,4,128,1]{2,1,0,3:T(4,128)(2,1)S(1)} %bitcast.146), kind=kOutput, calls=%fused_computation.30 | convolution fusion | flops 274989056 | bytes 5259776 | tf_op jit(solution)/shard_map/ikgj,jkd->ikgd/dot_general | solution.py:43
  54.9 13.4 %collective-permute-done.5 = bf16[256,1024]{1,0:T(8,128)(2,1)S(1)} collective-permute-done((bf16[256,1024]{1,0:T(8,128)(2,1)}, bf16[256,1024]{1,0:T(8,128)(2,1)S(1)}, u32[]{:S(2)}, u32[]{:S(2)}) %collective-permute-start.5) | collective-permute-done | bytes 524320 | tf_op jit(solution)/shard_map/ppermute | solution.py:67
  68.3 2.7 %fusion.2 = (f32[128,4,4]{0,2,1:T(4,128)S(1)}, f32[4,512,128,4]{2,1,3,0:T(8,128)}) fusion(pred[512]{0:T(512)(128)(4,1)S(1)} %get-tuple-element.24, bf16[128,4,4,128]{0,3,2,1:T(8,128)(2,1)S(1)} %bitcast.139, bf16[512,4,128,1]{2,1,0,3:T(4,128)(2,1)S(1)} %bitcast.141), kind=kOutput, calls=%fused_computation.11 | convolution fusion | flops 271579136 | bytes 5251584 | tf_op jit(solution)/shard_map/ikgd,jkd->ikgj/dot_general | solution.py:36
  71.2 4.8 %collective-permute-start.9 = (bf16[256,1024]{1,0:T(8,128)(2,1)}, bf16[256,1024]{1,0:T(8,128)(2,1)}, u32[]{:S(2)}, u32[]{:S(2)}) collective-permute-start(bf16[256,1024]{1,0:T(8,128)(2,1)} %collective-permute-done.8), channel_id=1, source_target_pairs={{2,0},{4,2},{6,4},{8,6},{10,8},{12,10},{14,12},{0,14},{3,1},{5,3},... | collective-permute-start | bytes 1572872 | tf_op jit(solution)/shard_map/ppermute | solution.py:72
  75.9 3.2 %fusion.15 = f32[128,4,4]{0,2,1:T(4,128)S(1)} fusion(f32[4,512,128,4]{2,1,3,0:T(8,128)} %get-tuple-element.26, f32[128,4,4]{0,2,1:T(4,128)S(1)} %get-tuple-element.25, pred[512]{0:T(512)(128)(4,1)S(1)} %get-tuple-element.24), kind=kLoop, calls=%fused_computation.26 | loop fusion | flops 5240832 | bytes 4211200 | tf_op jit(solution)/shard_map/reduce_sum | solution.py:42
  79.2 10.1 %collective-permute-done.6 = bf16[256,1024]{1,0:T(8,128)(2,1)} collective-permute-done((bf16[256,1024]{1,0:T(8,128)(2,1)S(1)}, bf16[256,1024]{1,0:T(8,128)(2,1)}, u32[]{:S(2)}, u32[]{:S(2)}) %collective-permute-start.6) | collective-permute-done | bytes 524320 | tf_op jit(solution)/shard_map/ppermute | solution.py:67
  89.3 2.6 %collective-permute-start.7 = (bf16[256,1024]{1,0:T(8,128)(2,1)}, bf16[256,1024]{1,0:T(8,128)(2,1)}, u32[]{:S(2)}, u32[]{:S(2)}) collective-permute-start(bf16[256,1024]{1,0:T(8,128)(2,1)} %collective-permute-done.6), channel_id=1, source_target_pairs={{0,2},{2,4},{4,6},{6,8},{8,10},{10,12},{12,14},{14,0},{1,3},{3,5},... | collective-permute-start | bytes 1572872 | tf_op jit(solution)/shard_map/ppermute | solution.py:67
  91.9 1.4 fusion.18
  94.3 13.2 %collective-permute-start.10 = (bf16[256,1024]{1,0:T(8,128)(2,1)}, bf16[256,1024]{1,0:T(8,128)(2,1)S(1)}, u32[]{:S(2)}, u32[]{:S(2)}) collective-permute-start(bf16[256,1024]{1,0:T(8,128)(2,1)} %collective-permute-done.9), channel_id=1, source_target_pairs={{2,0},{4,2},{6,4},{8,6},{10,8},{12,10},{14,12},{0,14},{3,1},{5,3},... | collective-permute-start | bytes 1572872 | tf_op jit(solution)/shard_map/ppermute | solution.py:72
  107.5 4.9 %collective-permute-done.7 = bf16[256,1024]{1,0:T(8,128)(2,1)} collective-permute-done((bf16[256,1024]{1,0:T(8,128)(2,1)}, bf16[256,1024]{1,0:T(8,128)(2,1)}, u32[]{:S(2)}, u32[]{:S(2)}) %collective-permute-start.7) | collective-permute-done | bytes 524320 | tf_op jit(solution)/shard_map/ppermute | solution.py:67
  112.4 1.9 %bitcast_dynamic-update-slice_fusion.7 = bf16[8,256,1024]{2,1,0:T(8,128)(2,1)} fusion(bf16[256,1024]{1,0:T(8,128)(2,1)} %collective-permute-done.7), kind=kLoop, calls=%fused_computation.53 | loop fusion | bytes 1048576
  114.2 1.9 %bitcast_dynamic-update-slice_fusion.6 = bf16[8,256,1024]{2,1,0:T(8,128)(2,1)} fusion(bf16[8,256,1024]{2,1,0:T(8,128)(2,1)} %bitcast_dynamic-update-slice_fusion.7, bf16[256,1024]{1,0:T(8,128)(2,1)} %collective-permute-done.6), kind=kLoop, calls=%fused_computation.52 | loop fusion | bytes 1048576
  117.0 1.9 %bitcast_dynamic-update-slice_fusion.4 = bf16[8,256,1024]{2,1,0:T(8,128)(2,1)} fusion(bf16[8,256,1024]{2,1,0:T(8,128)(2,1)} %bitcast_dynamic-update-slice_fusion.5, bf16[256,1024]{1,0:T(8,128)(2,1)} %collective-permute-done.4), kind=kLoop, calls=%fused_computation.50 | loop fusion | bytes 1048576
  119.7 1.9 %bitcast_dynamic-update-slice_fusion.2 = bf16[8,256,1024]{2,1,0:T(8,128)(2,1)} fusion(bf16[8,256,1024]{2,1,0:T(8,128)(2,1)} %bitcast_dynamic-update-slice_fusion.3, bf16[256,1024]{1,0:T(8,128)(2,1)} %collective-permute-done.8), kind=kLoop, calls=%fused_computation.48 | loop fusion | bytes 1048576
  121.6 1.9 %bitcast_dynamic-update-slice_fusion.1 = bf16[8,256,1024]{2,1,0:T(8,128)(2,1)} fusion(bf16[8,256,1024]{2,1,0:T(8,128)(2,1)} %bitcast_dynamic-update-slice_fusion.2, bf16[256,1024]{1,0:T(8,128)(2,1)} %collective-permute-done.9), kind=kLoop, calls=%fused_computation.47 | loop fusion | bytes 1048576
  124.3 5.0 %gather_fusion = bf16[8,256,1024]{2,1,0:T(8,128)(2,1)} fusion(bf16[8,256,1024]{2,1,0:T(8,128)(2,1)} %bitcast_dynamic-update-slice_fusion, s32[1024]{0:T(1024)S(1)} %pad_clamp_fusion), kind=kCustom, calls=%fused_computation | custom fusion | bytes 8388640 | tf_op jit(solution)/shard_map/gather | solution.py:80
  129.3 3.4 %convolution_convert_fusion = bf16[256,1024]{1,0:T(8,128)(2,1)S(1)} fusion(bf16[256,2048]{1,0:T(8,128)(2,1)S(1)} %bitcast.143, bf16[2048,1024]{1,0:T(8,128)(2,1)} %bitcast.137), kind=kOutput, calls=%fused_computation.31 | convolution fusion | flops 1074003968 | bytes 5767168 | tf_op jit(solution)/shard_map/dot_general | solution.py:119
  133.1 4.2 %all_to_all.4 = bf16[2,128,1024]{1,0,2:T(2,128)(2,1)S(1)} all-to-all(bf16[2,128,1024]{1,0,2:T(2,128)(2,1)S(1)} %copy.44), channel_id=1, replica_groups=mesh['clip'=2,'tm'=8,'tile'=2] {'tile'}, dimensions={2} | all-to-all | bytes 1048576 | tf_op jit(solution)/shard_map/all_to_all | solution.py:125
  140.8 1.6 %bitcast_reduce_fusion.1 = (f32[256,8]{0,1:T(8,128)S(1)}, f32[8,768,256]{2,1,0:T(8,128)S(1)}) fusion(pred[768]{0:T(1024)(128)(4,1)S(1)} %pad_add_fusion, bf16[256,8,64]{0,2,1:T(8,128)(2,1)S(1)} %get-tuple-element.13, bf16[256,8,64]{0,2,1:T(8,128)(2,1)S(1)} %bitcast.153), kind=kOutput, calls=%fused_computation.5 | convolution fusion | flops 208402432 | bytes 6824704 | tf_op jit(solution)/shard_map/ihd,jhd->ihj/dot_general | solution.py:147
  142.4 1.5 fusion.23
  144.1 1.6 %bitcast_reduce_fusion = (f32[256,8]{0,1:T(8,128)S(1)}, f32[8,768,256]{2,1,0:T(8,128)S(1)}) fusion(pred[768]{0:T(1024)(128)(4,1)S(1)} %pad_add_fusion.1, bf16[256,8,64]{0,2,1:T(8,128)(2,1)S(1)} %get-tuple-element.14, bf16[256,8,64]{0,2,1:T(8,128)(2,1)S(1)} %bitcast.151), kind=kOutput, calls=%fused_computation.2 | convolution fusion | flops 208402432 | bytes 6824704 | tf_op jit(solution)/shard_map/ihd,jhd->ihj/dot_general | solution.py:147
  145.7 1.5 %fusion.20 = bf16[8,64,256]{2,1,0:T(8,128)(2,1)S(1)} fusion(f32[8,768,256]{2,1,0:T(8,128)S(1)} %get-tuple-element.30, f32[256,8]{0,1:T(8,128)S(1)} %get-tuple-element.29, pred[768]{0:T(1024)(128)(4,1)S(1)} %pad_add_fusion.1, bf16[256,8,64]{0,2,1:T(8,128)(2,1)S(1)} %bitcast.152, bf16[256,8,64]{0,2,1:T(8,128)(2,1)S(1)} %get-tuple-element.14), kind=kOutput, calls=%fused_computation.32 | convolution fusion | flops 210108416 | bytes 7086848 | tf_op jit(solution)/shard_map/ihj,jhd->ihd/dot_general | solution.py:152
  (70 shorter events, 20.2 us)
Async XLA Ops:
  0.0 29.1 %copy-start.5 = (s32[2]{0:T(128)S(1)}, s32[2]{0:T(128)}, u32[]{:S(2)}) copy-start(s32[2]{0:T(128)} %param.9) | copy-start | bytes 28
  0.0 42.2 %copy-start.2 = (bf16[2,2,128,512]{3,2,1,0:T(8,128)(2,1)S(1)}, bf16[2,2,128,512]{3,2,1,0:T(8,128)(2,1)}, u32[]{:S(2)}) copy-start(bf16[2,2,128,512]{3,2,1,0:T(8,128)(2,1)} %param.6) | copy-start | bytes 1572868
  0.0 21.2 %copy-start.4 = (f32[512]{0:T(512)S(1)}, f32[512]{0:T(512)}, u32[]{:S(2)}) copy-start(f32[512]{0:T(512)} %param.8) | copy-start | bytes 6148
  0.0 27.7 %collective-permute-start.3 = (s32[2]{0:T(128)}, s32[2]{0:T(128)S(1)}, u32[]{:S(2)}, u32[]{:S(2)}) collective-permute-start(s32[2]{0:T(128)} %param.9), channel_id=1, source_target_pairs={{0,2},{2,4},{4,6},{6,8},{8,10},{10,12},{12,14},{1,3},{3,5},{5,7},{... | collective-permute-start | bytes 32 | tf_op jit(solution)/shard_map/ppermute | solution.py:28
  5.0 16.8 %collective-permute-start.12 = (s32[2]{0:T(128)}, s32[2]{0:T(128)S(1)}, u32[]{:S(2)}, u32[]{:S(2)}) collective-permute-start(s32[2]{0:T(128)} %param.9), channel_id=1, source_target_pairs={} | collective-permute-start | bytes 32 | tf_op jit(solution)/shard_map/ppermute | solution.py:28
  5.7 36.4 %collective-permute-start.1 = (bf16[2,2,128,512]{3,2,1,0:T(8,128)(2,1)}, bf16[2,2,128,512]{3,2,1,0:T(8,128)(2,1)S(1)}, u32[]{:S(2)}, u32[]{:S(2)}) collective-permute-start(bf16[2,2,128,512]{3,2,1,0:T(8,128)(2,1)} %param.6), channel_id=1, source_target_pairs={{0,2},{2,4},{4,6},{6,8},{8,10},{10,12},{12,14},{1,3},{3,5},{5,7},{... | collective-permute-start | bytes 1572872 | tf_op jit(solution)/shard_map/ppermute | solution.py:28
  10.5 18.7 %collective-permute-start.2 = (s32[1]{0:T(128)}, s32[1]{0:T(128)}, u32[]{:S(2)}, u32[]{:S(2)}) collective-permute-start(s32[1]{0:T(128)} %get-tuple-element.20), channel_id=1, source_target_pairs={{0,4},{2,6},{4,8},{6,10},{8,12},{10,14},{1,5},{3,7},{5,9},{7,11},{... | collective-permute-start | bytes 20 | tf_op jit(solution)/shard_map/ppermute | solution.py:28
  16.9 35.6 %collective-permute-start.4 = (bf16[256,1024]{1,0:T(8,128)(2,1)S(1)}, bf16[256,1024]{1,0:T(8,128)(2,1)}, u32[]{:S(2)}, u32[]{:S(2)}) collective-permute-start(bf16[256,1024]{1,0:T(8,128)(2,1)S(1)} %all_gather.3), channel_id=1, source_target_pairs={{0,2},{2,4},{4,6},{6,8},{8,10},{10,12},{12,14},{14,0},{1,3},{3,5},... | collective-permute-start | bytes 1572872 | tf_op jit(solution)/shard_map/ppermute | solution.py:67
  21.9 49.3 %collective-permute-start.8 = (bf16[256,1024]{1,0:T(8,128)(2,1)S(1)}, bf16[256,1024]{1,0:T(8,128)(2,1)}, u32[]{:S(2)}, u32[]{:S(2)}) collective-permute-start(bf16[256,1024]{1,0:T(8,128)(2,1)S(1)} %all_gather.3), channel_id=1, source_target_pairs={{2,0},{4,2},{6,4},{8,6},{10,8},{12,10},{14,12},{0,14},{3,1},{5,3},... | collective-permute-start | bytes 1572872 | tf_op jit(solution)/shard_map/ppermute | solution.py:72
  27.8 14.3 %collective-permute-start = (bf16[2,1,128,512]{3,2,1,0:T(8,128)(2,1)S(1)}, bf16[2,1,128,512]{3,2,1,0:T(8,128)(2,1)S(1)}, u32[]{:S(2)}, u32[]{:S(2)}) collective-permute-start(bf16[2,1,128,512]{3,2,1,0:T(8,128)(2,1)S(1)} %slice.65), channel_id=1, source_target_pairs={{0,4},{2,6},{4,8},{6,10},{8,12},{10,14},{1,5},{3,7},{5,9},{7,11},{... | collective-permute-start | bytes 786440 | tf_op jit(solution)/shard_map/ppermute | solution.py:28
  49.1 3.5 %copy-start.1 = (f32[4,512,128,4]{2,1,3,0:T(8,128)S(1)}, f32[4,512,128,4]{2,1,3,0:T(8,128)}, u32[]{:S(2)}) copy-start(f32[4,512,128,4]{2,1,3,0:T(8,128)} %get-tuple-element.28) | copy-start | bytes 12582916
  52.5 15.8 %collective-permute-start.5 = (bf16[256,1024]{1,0:T(8,128)(2,1)}, bf16[256,1024]{1,0:T(8,128)(2,1)S(1)}, u32[]{:S(2)}, u32[]{:S(2)}) collective-permute-start(bf16[256,1024]{1,0:T(8,128)(2,1)} %collective-permute-done.4), channel_id=1, source_target_pairs={{0,2},{2,4},{4,6},{6,8},{8,10},{10,12},{12,14},{14,0},{1,3},{3,5},... | collective-permute-start | bytes 1572872 | tf_op jit(solution)/shard_map/ppermute | solution.py:67
  68.3 21.0 %collective-permute-start.6 = (bf16[256,1024]{1,0:T(8,128)(2,1)S(1)}, bf16[256,1024]{1,0:T(8,128)(2,1)}, u32[]{:S(2)}, u32[]{:S(2)}) collective-permute-start(bf16[256,1024]{1,0:T(8,128)(2,1)S(1)} %collective-permute-done.5), channel_id=1, source_target_pairs={{0,2},{2,4},{4,6},{6,8},{8,10},{10,12},{12,14},{14,0},{1,3},{3,5},... | collective-permute-start | bytes 1572872 | tf_op jit(solution)/shard_map/ppermute | solution.py:67
  71.1 20.8 %copy-start = (f32[4,512,128,4]{2,1,3,0:T(8,128)S(1)}, f32[4,512,128,4]{2,1,3,0:T(8,128)}, u32[]{:S(2)}) copy-start(f32[4,512,128,4]{2,1,3,0:T(8,128)} %get-tuple-element.26) | copy-start | bytes 12582916
  71.2 23.1 %collective-permute-start.9 = (bf16[256,1024]{1,0:T(8,128)(2,1)}, bf16[256,1024]{1,0:T(8,128)(2,1)}, u32[]{:S(2)}, u32[]{:S(2)}) collective-permute-start(bf16[256,1024]{1,0:T(8,128)(2,1)} %collective-permute-done.8), channel_id=1, source_target_pairs={{2,0},{4,2},{6,4},{8,6},{10,8},{12,10},{14,12},{0,14},{3,1},{5,3},... | collective-permute-start | bytes 1572872 | tf_op jit(solution)/shard_map/ppermute | solution.py:72
  89.3 23.0 %collective-permute-start.7 = (bf16[256,1024]{1,0:T(8,128)(2,1)}, bf16[256,1024]{1,0:T(8,128)(2,1)}, u32[]{:S(2)}, u32[]{:S(2)}) collective-permute-start(bf16[256,1024]{1,0:T(8,128)(2,1)} %collective-permute-done.6), channel_id=1, source_target_pairs={{0,2},{2,4},{4,6},{6,8},{8,10},{10,12},{12,14},{14,0},{1,3},{3,5},... | collective-permute-start | bytes 1572872 | tf_op jit(solution)/shard_map/ppermute | solution.py:67
  91.9 1.4 copy-start.3
  94.3 29.2 %collective-permute-start.10 = (bf16[256,1024]{1,0:T(8,128)(2,1)}, bf16[256,1024]{1,0:T(8,128)(2,1)S(1)}, u32[]{:S(2)}, u32[]{:S(2)}) collective-permute-start(bf16[256,1024]{1,0:T(8,128)(2,1)} %collective-permute-done.9), channel_id=1, source_target_pairs={{2,0},{4,2},{6,4},{8,6},{10,8},{12,10},{14,12},{0,14},{3,1},{5,3},... | collective-permute-start | bytes 1572872 | tf_op jit(solution)/shard_map/ppermute | solution.py:72
  139.8 0.9 collective-permute-start.11
